TPU v7x, 32 devices: a whole 2x2x4 slice. The times are simulated.
32 devices in a mesh: focus: 2 (over y), tx: 4 (over z), ty: 2 (over core), dose: 2 (over x).
Axes of the slice: x: 2, y: 2, z: 4, core: 2. Of those that a mesh axis runs over, the one named last changes fastest.
Arguments:
- aerial_image: float32 [64, 32, 256], P('focus', 'tx', 'ty'), parts along dimension 0, may hold values from 0.2 to 2
- quencher: float32 [32, 32, 256], P(None, 'tx', 'ty'), may hold values from 0.1 to 0.8
- cotangent: float32 [8, 32, 32, 256], P(('focus', 'dose'), None, 'tx', 'ty'), parts along dimension 0, may hold values from -6 to 6
- dose_levels: float32 [16], replicated, may hold values from 0.5 to 2
- dose_index: int32 [8], P(('focus', 'dose')), parts along dimension 0, may hold values from 0 to 15
Outputs:
- image_grad: float32 [64, 32, 256], P(('focus', 'dose'), 'tx', 'ty'), parts along dimension 0
There are 2 independent parts, one for each index of `focus`. A program takes and returns all parts, laid end to end along the dimension named above; an argument that names none is the same for every part. Nothing has to cross between parts.
All inputs are finite; a program needn't handle non-finite values.
Results may differ from a plain program's by a relative error of at most 0.00002.
Values sent between devices are 32-bit elements; how exact they have to be, the bound alone decides.
No kernel may reach another device: no remote copies, remote signals or barrier semaphores. Data moves between devices by JAX's collectives and lax.ppermute only.
A program may use at most 64 MiB of HBM per device.

v0:
```python
import jax
import jax.numpy as jnp
from jax import lax
from jax.experimental import pallas as pl
from jax.experimental.pallas import tpu as pltpu
from jax.sharding import PartitionSpec as P


exposure_rate = 1.0
neutral_rate = 0.8
deprotect_rate = 0.5
acid_lateral = 0.23
acid_depth = 0.02
base_lateral = 0.2
base_depth = 0.02

HALO_AERIAL = 5
HALO_QUENCH = 4
HALO_COT = 3
SUB = 8
LIMIT = 20 << 20


class Window:
    def __init__(self, depth, doses):
        self.depth, self.doses = depth, doses
        self.piece = depth // doses
        self.ends = 0 if doses == 1 else 1 if doses == 2 else 2
        self.size = min(depth, self.piece + SUB * self.ends)
        self.groups = self.size // SUB

    def layers(self, halo):
        return min(self.depth, self.piece + halo * self.ends)

    def clamp(self, owner, halo, size):
        return jnp.minimum(jnp.maximum(owner * self.piece - halo, 0), self.depth - size)

    def start(self, owner):
        return self.clamp(owner, SUB, self.size)

    def sent(self, owner, halo):
        return self.clamp(owner, halo, self.layers(halo))


class Dense:
    def __init__(self, window, reaches, lead=True, tail=True, size=0):
        self.window = window
        slack = [window.size - window.layers(reach) for reach in reaches]
        used = sum(window.layers(reach) for reach in reaches)
        ends = (slack[0] if lead else 0) + (slack[-1] if tail else 0)
        self.size = max(size, -(-(used + ends) // SUB) * SUB)
        at = self.size - used if lead and not tail else slack[0] if lead else 0
        self.rows = []
        for reach in reaches:
            self.rows.append((at, reach))
            at += window.layers(reach)

    def put(self, dst, i, src, base, rows, row, owner, block=0):
        at, reach = self.rows[i]
        first, layers = self.window.sent(owner, reach), self.window.layers(reach)
        for g in range(0, layers, SUB):
            n = min(SUB, layers - g)
            value = src[pl.ds(base + rows * (first + g) + row, n, stride=rows), :]
            dst[pl.ds(block + at + g, n), :] = value

    def get(self, src, i, owner, block=0):
        at, reach = self.rows[i]
        window = self.window
        start = block + at - (window.sent(owner, reach) - window.start(owner))
        return [src[pl.ds(start + k, SUB, stride=window.groups), :] for k in range(window.groups)]


def clear(dst, at, size):
    dst[pl.ds(at, size), :] = jnp.zeros((size, dst.shape[1]), jnp.float32)


def image_layout(window):
    aerial = [HALO_AERIAL - i for i in range(1, HALO_AERIAL + 1)]
    quench = [HALO_QUENCH - i for i in range(HALO_QUENCH, 0, -1)]
    return Dense(window, aerial + quench)


def crosses(k):
    return k % 2 == 1


def halo_layouts(window, local):
    reaches = [HALO_COT - i for _ in range(local) for i in range(1, HALO_COT + 1)]
    size = Dense(window, reaches, lead=False).size
    first = Dense(window, reaches, tail=False, size=size)
    return first, Dense(window, reaches, lead=False, size=first.size)


def whole_layout(rows, window, local):
    return Dense(window, [HALO_COT] * (local * rows))


def chip_row(rows, row):
    return row + lax.axis_index("ty") * (rows - 1 - 2 * row)


def vector(ref, rows, groups, first, row, base=0):
    return ref[pl.ds(base + rows * first + row, SUB, stride=rows * groups), :]


def image_kernel(rows, window, local, *refs):
    image_hbm, quench_hbm, cot_hbm, levels_hbm, index_hbm = refs[:5]
    image_s, image_c, dose, aerial, quench, cot, levels, index, sems = refs[5:]
    pairs = ((image_hbm, aerial), (quench_hbm, quench), (cot_hbm, cot), (levels_hbm, levels), (index_hbm, index))
    copies = [pltpu.make_async_copy(src, dst, sems.at[i]) for i, (src, dst) in enumerate(pairs)]
    for copy in copies:
        copy.start()
    layout = image_layout(window)
    for ref in (image_s, image_c):
        clear(ref, 0, SUB)
        clear(ref, layout.size - 2 * SUB, 2 * SUB)
    owner = lax.axis_index("dose")
    copies[0].wait()
    copies[1].wait()
    order = [(aerial, i) for i in range(1, HALO_AERIAL + 1)]
    order += [(quench, i) for i in range(HALO_QUENCH, 0, -1)]
    for place, (src, i) in enumerate(order):
        layout.put(image_s, place, src, 0, rows, chip_row(rows, rows - i), owner)
        layout.put(image_c, place, src, 0, rows, chip_row(rows, i - 1), owner)
    for copy in copies[2:]:
        copy.wait()
    for d in range(local):
        dose[d] = jnp.full(dose.shape[1:], levels[index[d]], jnp.float32)


def swap_layout(rows, window, local):
    vectors = 2 * rows + local * (rows // 2 + HALO_COT)
    return vectors * window.groups * SUB, halo_layouts(window, local)[0].size


def swapped(swap, groups, place):
    return [swap[pl.ds((place * groups + k) * SUB, SUB), :] for k in range(groups)]


def rest_kernel(rows, window, local, aerial, quench, cot, swap, *dense):
    depth, groups, doses = window.depth, window.groups, window.doses
    area = rows * depth
    inner = rows // 2 + HALO_COT
    owner = lax.axis_index("dose")
    sends = dense[:doses]
    wholes = dense[doses:]
    handed, halo = swap_layout(rows, window, local)
    layouts = halo_layouts(window, local)
    whole = whole_layout(rows, window, local)
    for k in range(doses):
        target = lax.rem(owner + k, doses)
        block = handed + k * halo
        mine, given = layouts[::-1] if crosses(k) else layouts
        for ref, at in ((sends[k], 0), (swap, block)):
            clear(ref, at, 2 * SUB)
            clear(ref, at + halo - 2 * SUB, 2 * SUB)
        for d in range(local):
            for i in range(1, HALO_COT + 1):
                outer, inward = chip_row(rows, rows - i), chip_row(rows, i - 1)
                if crosses(k):
                    outer, inward = inward, outer
                place = d * HALO_COT + i - 1
                mine.put(sends[k], place, cot, d * area, rows, outer, target)
                given.put(swap, place, cot, d * area, rows, inward, target, block)
        if k:
            ref = wholes[k - 1]
            clear(ref, 0, SUB)
            clear(ref, whole.size - 2 * SUB, 2 * SUB)
            for d in range(local):
                for row in range(rows):
                    whole.put(ref, d * rows + row, cot, d * area, rows, row, target)
    place = 0
    parts = [(aerial, 0, rows), (quench, 0, rows)] + [(cot, d * area, inner) for d in range(local)]
    start = window.start(owner)
    for src, base, width in parts:
        for i in range(width):
            for k in range(groups):
                value = vector(src, rows, groups, start + k, chip_row(rows, rows - 1 - i), base)
                swap[pl.ds((place * groups + k) * SUB, SUB), :] = value
            place += 1


def make_spread():
    lane = lax.broadcasted_iota(jnp.int32, (SUB, 128), 1)
    sub = lax.broadcasted_iota(jnp.int32, (SUB, 128), 0)
    first_lane = lane == 0
    last_lane = lane == 127
    first_sub = sub == 0
    last_sub = sub == SUB - 1

    def spread(above, center, below, along, depthwise, loss=None):
        count = len(center)
        groups = count // 2
        keep = 1.0 - 4.0 * along - 2.0 * depthwise
        result = []
        for i in range(count):
            k = i % groups
            j = (i + groups) % count
            right = pltpu.roll(jnp.where(first_lane, center[j], center[i]), 127, 1)
            left = pltpu.roll(jnp.where(last_lane, center[j], center[i]), 1, 1)
            lateral = (above[i] + below[i]) + (right + left)
            if k + 1 < groups:
                deeper = center[i + 1]
            else:
                deeper = jnp.where(last_sub, center[i], pltpu.roll(center[i - k], SUB - 1, 0))
            if k > 0:
                higher = center[i - 1]
            else:
                higher = jnp.where(first_sub, center[i], pltpu.roll(center[i + groups - 1], 1, 0))
            kept = (keep if loss is None else keep - loss[i]) * center[i]
            result.append(kept + along * lateral + depthwise * (deeper + higher))
        return result

    return spread


def near_rows(rows):
    half = rows // 2
    return {
        "q0": (0, rows),
        "a0": (0, rows),
        "a1": (1, rows - 1),
        "a2": (2, rows - 2),
        "a3": (3, rows - 3),
        "q1": (1, rows - 1),
        "q2": (2, rows - 2),
        "c3": (2, half + 3),
        "c2": (3, half + 2),
        "c1": (3, half + 1),
        "c0": (3, half),
        "e": (0, half),
        "dose": (0, 1),
    }


def far_rows(rows):
    return {
        "q0": (-4, 0),
        "a0": (-5, 0),
        "a1": (-4, 1),
        "a2": (-3, 2),
        "a3": (-2, 3),
        "q1": (-3, 1),
        "q2": (-2, 2),
        "c3": (-3, 2),
        "c2": (-2, 3),
        "c1": (-1, 3),
        "c0": (0, 3),
    }


def places_of(table, local):
    places, total = {}, 0
    for name, (first, end) in table.items():
        for d in range(local):
            for row in range(first, end):
                if name == "q0" and d > 0:
                    places[name, d, row] = places[name, 0, row]
                else:
                    places[name, d, row] = total
                    total += 1
    return places, total


def back_near_rows(rows):
    half = rows // 2
    return {
        "ct": (0, half + 3),
        "l3": (0, half + 3),
        "l2": (1, half + 2),
        "m2": (0, half + 1),
        "l1": (2, half + 1),
        "m1": (1, half),
        "g": (3, half),
    }


def back_far_rows(rows):
    return {
        "ct": (-3, 0),
        "l3": (-3, 0),
        "l2": (-2, 1),
        "m2": (-1, 0),
        "l1": (-1, 2),
        "m1": (0, 1),
        "g": (0, 3),
    }


class Fields:
    def __init__(self, rows, *stores):
        self.stores = [(ref, places_of(table(rows), count)[0], first) for ref, table, first, count in stores]
        self.more = {}

    def get(self, name, d, row):
        if (name, d, row) in self.more:
            return self.more[name, d, row]
        for ref, places, first in self.stores:
            if (name, d - first, row) in places:
                at = places[name, d - first, row]
                return [ref[at, i] for i in range(ref.shape[1])]
        raise KeyError((name, row))

    def around(self, name, d, row):
        return [self.get(name, d, row + i) for i in (-1, 0, 1)]

    def put(self, name, d, row, value):
        ref, places, first = self.stores[-1]
        at = places[name, d - first, row]
        for i in range(len(value)):
            ref[at, i] = value[i]


def left_of(acid):
    return [1.0 - (deprotect_rate / neutral_rate) * v for v in acid]


def next_acid(spread, fields, d, n, row):
    quench = fields.get("q%d" % n, d, row)
    return spread(*fields.around("a%d" % n, d, row), acid_lateral, acid_depth, quench)


def forward_rows(spread, fields, d, table):
    for n in range(3):
        first, end = table["a%d" % (n + 1)]
        for row in range(first, end):
            fields.put("a%d" % (n + 1), d, row, next_acid(spread, fields, d, n, row))
            if n < 2:
                q_first, q_end = table["q%d" % (n + 1)]
                if q_first <= row < q_end:
                    name = "q%d" % n
                    acid = fields.get("a%d" % n, d, row)
                    new = spread(*fields.around(name, d, row), base_lateral, base_depth, acid)
                    fields.put("q%d" % (n + 1), d, row, new)

    first = min(table[c][0] for c in ("c3", "c2", "c1", "c0"))
    end = max(table[c][1] for c in ("c3", "c2", "c1", "c0"))
    for row in range(first, end):
        wanted = [n for n in range(4) if table["c%d" % n][0] <= row < table["c%d" % n][1]]
        left = {}

        def of(n):
            if n not in left:
                left[n] = left_of(fields.get("a%d" % n, d, row))
            return left[n]

        for n in wanted:
            parts = [m for m in range(4) if m != n]
            if n >= 2 and table["e"][1] > 0 and row == table["c%d" % n][1] - 1:
                parts = parts[:2]
            value = [(-deprotect_rate) * v for v in of(parts[0])]
            for m in parts[1:]:
                value = [v * w for v, w in zip(value, of(m))]
            fields.put("c%d" % n, d, row, value)


def near_kernel(rows, window, local, *refs):
    doses, groups = window.doses, window.groups
    dose_refs, (aerial, quench, swap, near) = refs[:doses], refs[doses:]
    half = rows // 2
    spread = make_spread()
    total = local * doses
    fields = Fields(rows, (near, near_rows, 0, total))
    start = window.start(lax.axis_index("dose"))

    def source(raw, at, row):
        own = [vector(raw, rows, groups, start + k, chip_row(rows, row)) for k in range(groups)]
        return own + swapped(swap, groups, at + row)

    for row in range(rows):
        fields.put("q0", 0, row, [neutral_rate * v for v in source(quench, rows, row)])
    for d in range(total):
        dose = dose_refs[d // local][d % local]
        fields.put("dose", d, 0, [dose] * (2 * groups))
        rate = -exposure_rate * dose
        for row in range(rows):
            absorbed = [jnp.exp(rate * v) for v in source(aerial, 0, row)]
            fields.put("a0", d, row, [neutral_rate - neutral_rate * v for v in absorbed])
            if row < half:
                fields.put("e", d, row, [exposure_rate * dose * v for v in absorbed])
        forward_rows(spread, fields, d, near_rows(rows))


def far_kernel(rows, window, total, near, image_s, image_c, far):
    spread = make_spread()
    fields = Fields(rows, (near, near_rows, 0, total), (far, far_rows, 0, total))
    table = dict(far_rows(rows), e=(0, 0))
    owner = lax.axis_index("dose")
    layout = image_layout(window)

    def source(place):
        return [v for src in (image_s, image_c) for v in layout.get(src, place, owner)]

    for row in range(-HALO_QUENCH, 0):
        fields.put("q0", 0, row, [neutral_rate * v for v in source(HALO_AERIAL + HALO_QUENCH + row)])
    for d in range(total):
        rate = -exposure_rate * fields.get("dose", d, 0)[0]
        for row in range(-HALO_AERIAL, 0):
            absorbed = [jnp.exp(rate * v) for v in source(-1 - row)]
            fields.put("a0", d, row, [neutral_rate - neutral_rate * v for v in absorbed])
        forward_rows(spread, fields, d, table)


def backward_rows(spread, past, back, d, table):
    def step(name, row, other, n):
        quench = past.get("q%d" % n, d, row)
        new = spread(*back.around(name, d, row), acid_lateral, acid_depth, quench)
        if other is not None:
            new = [v - q * m for v, q, m in zip(new, quench, other)]
        return [v + c * t for v, c, t in zip(new, past.get("c%d" % n, d, row), back.get("ct", d, row))]

    for row in range(*table["l3"]):
        back.put("l3", d, row, [c * v for c, v in zip(past.get("c3", d, row), back.get("ct", d, row))])
    for row in range(*table["m2"]):
        parts = zip(past.get("a2", d, row), back.get("l3", d, row))
        back.put("m2", d, row, [-(a * s) for a, s in parts])
    for row in range(*table["l2"]):
        back.put("l2", d, row, step("l3", row, None, 2))
    for n, name in ((1, "l1"), (0, "g")):
        old, side = ("l2", "m2") if n else ("l1", "m1")
        wanted = set(range(*table[name]))
        if n:
            wanted |= set(range(*table["m1"]))
        for row in sorted(wanted):
            other = back.get(side, d, row)
            if row in range(*table[name]):
                new = step(old, row, other, n)
                if n == 0:
                    new = [v * e for v, e in zip(new, past.get("e", d, row))]
                back.put(name, d, row, new)
            if n and row in range(*table["m1"]):
                acid = past.get("a1", d, row)
                new = spread(*back.around("m2", d, row), base_lateral, base_depth, acid)
                back.put("m1", d, row, [v - a * s for v, a, s in zip(new, acid, back.get(old, d, row))])


def back_near_kernel(rows, window, local, group, near, far, extra_own, extra_par, cot, swap, *refs):
    doses, groups = window.doses, window.groups
    wholes, back_near = refs[:-1], refs[-1]
    half = rows // 2
    area = rows * window.depth
    inner = half + HALO_COT
    total = local * doses
    spread = make_spread()
    owner = lax.axis_index("dose")
    start = window.start(owner)
    image = image_layout(window)
    whole = whole_layout(rows, window, local)
    for d in range(group * local, (group + 1) * local):
        past = Fields(rows, (near, near_rows, 0, total), (far, far_rows, 0, total))
        rate = -exposure_rate * past.get("dose", d, 0)[0]
        light = [v for src in (extra_own, extra_par) for v in image.get(src, 0, owner)]
        past.more["a0", d, rows] = [neutral_rate - neutral_rate * jnp.exp(rate * v) for v in light]
        for n in range(3):
            row = rows - 1 - n
            past.more["a%d" % (n + 1), d, row] = next_acid(spread, past, d, n, row)
        for n, row in ((3, half + 2), (2, half + 1)):
            left = left_of(past.get("a%d" % (5 - n), d, row))
            past.more["c%d" % n, d, row] = [v * m for v, m in zip(past.get("c%d" % n, d, row), left)]
        back = Fields(rows, (back_near, back_near_rows, group * local, local))
        table = back_near_rows(rows)
        i = d - group * local
        for row in range(*table["ct"]):
            if group == 0:
                value = [vector(cot, rows, groups, start + g, chip_row(rows, row), i * area) for g in range(groups)]
                value += swapped(swap, groups, 2 * rows + i * inner + row)
            else:
                at = chip_row(rows, row) * window.layers(HALO_COT)
                sides = wholes
                value = [v for src in sides for v in whole.get(src, i * rows, owner, at)]
            back.put("ct", d, row, value)
        backward_rows(spread, past, back, d, table)


def back_far_kernel(rows, window, local, near, far, *refs):
    doses, groups = window.doses, window.groups
    backs, refs = refs[:doses], refs[doses:]
    sends = refs[:doses]
    mine, other, store, full = refs[doses:]
    layouts = halo_layouts(window, local)
    half = rows // 2
    total = local * doses
    owner = lax.axis_index("dose")
    spread = make_spread()
    past = Fields(rows, (near, near_rows, 0, total), (far, far_rows, 0, total))
    stores = [(ref, back_near_rows, k * local, local) for k, ref in enumerate(backs)]
    back = Fields(rows, *stores, (store, back_far_rows, 0, total))
    table = back_far_rows(rows)
    for d in range(total):
        k, i = divmod(d, local)
        for row in range(*table["ct"]):
            place = i * HALO_COT - 1 - row
            value = layouts[0].get(sends[k], place, owner)
            back.put("ct", d, row, value + layouts[1].get(sends[k], place, owner, layouts[0].size))
        backward_rows(spread, past, back, d, table)
    for row in range(half):
        value = back.get("g", 0, row)
        for d in range(1, total):
            value = [v + w for v, w in zip(value, back.get("g", d, row))]
        for i in range(2 * groups):
            side, k = divmod(i, groups)
            full[side, row, pl.ds(k, SUB, stride=groups), :] = value[i]
    start = pl.multiple_of(owner * window.piece - window.start(owner), SUB)
    for side, out in enumerate((mine, other)):
        for row in range(half):
            out[row] = full[side, row, pl.ds(start, window.piece), :]


def join_kernel(rows, piece, mine, other, out):
    core = lax.axis_index("ty")
    for owner, part in ((core, mine), (1 - core, other)):
        for row in range(rows // 2):
            at = row + owner * (rows - 1 - 2 * row)
            for g in range(0, piece, SUB):
                out[pl.ds(g * rows + at, SUB, stride=rows), :] = part[row, pl.ds(g, SUB), :]


def gradient(aerial_image, quencher, cotangent, dose_levels, dose_index):
    depth, rows, lanes = aerial_image.shape
    local = cotangent.shape[0]
    half = rows // 2
    doses = lax.axis_size("dose")
    ring = lax.axis_size("tx")
    assert rows == half + HALO_QUENCH and HALO_AERIAL == HALO_QUENCH + 1
    window = Window(depth, doses)
    groups, piece = window.groups, window.piece
    total = local * doses
    f32 = jnp.float32
    aerial = aerial_image.reshape(depth * rows, lanes)
    quench = quencher.reshape(depth * rows, lanes)
    cot = cotangent.reshape(local * depth * rows, lanes)

    def call(kernel, fixed, args, outs, scratch=(), flops=0, space=pltpu.VMEM):
        def body(*refs):
            kernel(*fixed, *refs)

        moved = sum(4 * x.size for x in list(args) + list(outs))
        return pl.pallas_call(
            body,
            out_shape=tuple(outs),
            in_specs=[pl.BlockSpec(memory_space=space)] * len(args),
            out_specs=(pl.BlockSpec(memory_space=pltpu.VMEM),) * len(outs),
            scratch_shapes=list(scratch),
            compiler_params=pltpu.CompilerParams(vmem_limit_bytes=LIMIT),
            cost_estimate=pl.CostEstimate(flops=flops, bytes_accessed=moved, transcendentals=0),
        )(*args)

    def array(*shape):
        return jax.ShapeDtypeStruct(shape + (lanes,), f32)

    def store(table, count=total):
        return (places_of(table(rows), count)[1], 2 * groups, SUB)

    def along(value, cross=0, step=1, k=0):
        pairs = []
        for t in range(ring):
            for c in range(2):
                for d in range(doses):
                    up = step * (1 - 2 * (c ^ cross))
                    target = (((t + up) % ring) * 2 + (c ^ cross)) * doses + (d + k) % doses
                    pairs.append(((t * 2 + c) * doses + d, target))
        return lax.ppermute(value, ("tx", "ty", "dose"), pairs)

    def across(value):
        return along(value, cross=1, step=0)

    images = array(image_layout(window).size)
    handed, halo = swap_layout(rows, window, local)
    whole = array(whole_layout(rows, window, local).size)
    flat = [jax.ShapeDtypeStruct(x.shape, f32) for x in (aerial, quench, cot)]
    image_s, image_c, dose, aerial, quench, cot = call(
        image_kernel,
        (rows, window, local),
        [pltpu.with_memory_space_constraint(x, pltpu.HBM) for x in (aerial, quench, cot, dose_levels, dose_index)],
        [images, images, array(local, SUB)] + flat,
        [
            pltpu.SMEM(dose_levels.shape, f32),
            pltpu.SMEM(dose_index.shape, jnp.int32),
            pltpu.SemaphoreType.DMA((5,)),
        ],
        space=pltpu.HBM,
    )
    image_s = along(image_s)
    image_c = along(image_c, cross=1)
    rest = call(
        rest_kernel,
        (rows, window, local),
        (aerial, quench, cot),
        [array(handed + doses * halo)] + [array(halo)] * doses + [whole] * (doses - 1),
    )
    swap = across(rest[0])
    values, wholes = [dose], []
    for k in range(1, doses):
        arrived = along(rest[doses + k], step=0, k=k)
        values.append(along(dose, step=0, k=k))
        wholes.append([arrived, across(arrived)])
    sends = []
    for k in range(doses):
        other = lax.slice_in_dim(swap, handed + k * halo, handed + (k + 1) * halo)
        both = jnp.concatenate((other, rest[1 + k]) if crosses(k) else (rest[1 + k], other), axis=0)
        sends.append(along(both, cross=int(crosses(k)), k=k))

    (near,) = call(
        near_kernel, (rows, window, local), values + [aerial, quench, swap], [array(*store(near_rows))], flops=10_000_000
    )
    extra_own = across(image_c)
    extra_par = across(image_s)
    (far,) = call(
        far_kernel, (rows, window, total), (near, image_s, image_c), [array(*store(far_rows))], flops=10_000_000
    )
    backs = []
    for k in range(doses):
        backs += call(
            back_near_kernel,
            (rows, window, local, k),
            [near, far, extra_own, extra_par, cot, swap] + (wholes[k - 1] if k else []),
            [array(*store(back_near_rows, local))],
            flops=10_000_000,
        )
    mine, other = call(
        back_far_kernel,
        (rows, window, local),
        [near, far] + backs + sends,
        [array(half, piece)] * 2,
        [
            pltpu.VMEM(store(back_far_rows) + (lanes,), f32),
            pltpu.VMEM((2, half, window.size, lanes), f32),
        ],
        flops=10_000_000,
    )
    other = across(other)
    (out,) = call(join_kernel, (rows, piece), (mine, other), [array(piece * rows)])
    return out.reshape(piece, rows, lanes)


def solution(mesh):
    placed = (
        P("focus", "tx", "ty"),
        P(None, "tx", "ty"),
        P(("focus", "dose"), None, "tx", "ty"),
        P(),
        P(("focus", "dose")),
    )
    return jax.shard_map(
        gradient,
        mesh=mesh,
        in_specs=placed,
        out_specs=P(("focus", "dose"), "tx", "ty"),
        check_vma=False,
    )
```

profile of v0, /device:TPU:0, one launch (start us, length us, event | category | flops | bytes accessed | tf_op | source)
XLA Modules:
  0.0 23.3 jit_solution(577245734233567265)
XLA Ops:
  0.0 1.1 %shard_map.55 = (f32[176,128]{1,0:T(8,128)S(1)}, f32[176,128]{1,0:T(8,128)S(1)}, f32[2,8,128]{2,1,0:T(8,128)S(1)}, f32[256,128]{1,0:T(8,128)S(1)}, f32[256,128]{1,0:T(8,128)S(1)}, /*index=5*/f32[512,128]{1,0:T(8,128)S(1)}) custom-call(f32[256,128]{1,0:T(8,128)} %bitcast.5, f32[256,128]{1,0:T(8,128)} %bitcast.6, f32[512,128]{1,0:T(8,128)} %bitcast.4, ...), custom_call_target="tpu_custom_call" | custom-call | bytes 1237064 | tf_op jit(solution)/shard_map/pallas_call | solution.py:538
  1.2 0.2 shard_map.56
  1.3 0.6 %collective-permute-start.1 = (f32[944,128]{1,0:T(8,128)S(1)}, f32[944,128]{1,0:T(8,128)S(1)}, u32[]{:S(2)}, u32[]{:S(2)}) collective-permute-start(f32[944,128]{1,0:T(8,128)S(1)} %get-tuple-element.21), channel_id=1, source_target_pairs={{0,2},{1,3},{2,0},{3,1},{4,6},{5,7},{6,4},{7,5},{8,10},{9,11},{10,... | collective-permute-start | bytes 1449992 | tf_op jit(solution)/shard_map/ppermute | solution.py:562
  1.9 2.6 %collective-permute-start.6 = (f32[320,128]{1,0:T(8,128)S(1)}, f32[320,128]{1,0:T(8,128)S(1)}, u32[]{:S(2)}, u32[]{:S(2)}) collective-permute-start(f32[320,128]{1,0:T(8,128)S(1)} %get-tuple-element.24), channel_id=1, source_target_pairs={{0,1},{1,0},{2,3},{3,2},{4,5},{5,4},{6,7},{7,6},{8,9},{9,8},{10,11... | collective-permute-start | bytes 491528 | tf_op jit(solution)/shard_map/ppermute | solution.py:562
  4.4 0.1 collective-permute-start
  4.5 2.0 %collective-permute-start.2 = (f32[176,128]{1,0:T(8,128)S(1)}, f32[176,128]{1,0:T(8,128)S(1)}, u32[]{:S(2)}, u32[]{:S(2)}) collective-permute-start(f32[176,128]{1,0:T(8,128)S(1)} %get-tuple-element.22), channel_id=1, source_target_pairs={{0,4},{1,5},{2,14},{3,15},{4,8},{5,9},{6,2},{7,3},{8,12},{9,13},{1... | collective-permute-start | bytes 270344 | tf_op jit(solution)/shard_map/ppermute | solution.py:562
  6.5 1.7 %collective-permute-start.3 = (f32[176,128]{1,0:T(8,128)S(1)}, f32[176,128]{1,0:T(8,128)S(1)}, u32[]{:S(2)}, u32[]{:S(2)}) collective-permute-start(f32[176,128]{1,0:T(8,128)S(1)} %get-tuple-element.23), channel_id=1, source_target_pairs={{0,14},{1,15},{2,4},{3,5},{4,2},{5,3},{6,8},{7,9},{8,6},{9,7},{10,... | collective-permute-start | bytes 270344 | tf_op jit(solution)/shard_map/ppermute | solution.py:562
  8.2 1.1 %collective-permute-done.6.refs_6_ = f32[320,128]{1,0:T(8,128)S(1)} collective-permute-done((f32[320,128]{1,0:T(8,128)S(1)}, f32[320,128]{1,0:T(8,128)S(1)}, u32[]{:S(2)}, u32[]{:S(2)}) %collective-permute-start.6) | collective-permute-done | bytes 163872 | tf_op jit(solution)/shard_map/ppermute | solution.py:562
  9.3 0.0 collective-permute-start.7
  9.3 0.0 collective-permute-done.1.refs_4_.refs_5_
  9.4 1.9 %collective-permute-start.8 = (f32[224,128]{1,0:T(8,128)S(1)}, f32[224,128]{1,0:T(8,128)S(1)}, u32[]{:S(2)}, u32[]{:S(2)}) collective-permute-start(f32[224,128]{1,0:T(8,128)S(1)} %pad_maximum_fusion), channel_id=1, source_target_pairs={{0,4},{1,5},{2,14},{3,15},{4,8},{5,9},{6,2},{7,3},{8,12},{9,13},{1... | collective-permute-start | bytes 344072 | tf_op jit(solution)/shard_map/ppermute | solution.py:562
  11.2 0.0 collective-permute-done.refs_1_
  11.3 3.3 %collective-permute-start.9 = (f32[224,128]{1,0:T(8,128)S(1)}, f32[224,128]{1,0:T(8,128)S(1)}, u32[]{:S(2)}, u32[]{:S(2)}) collective-permute-start(f32[224,128]{1,0:T(8,128)S(1)} %pad_maximum_fusion.1), channel_id=1, source_target_pairs={{0,15},{1,14},{2,5},{3,4},{4,3},{5,2},{6,9},{7,8},{8,7},{9,6},{10,... | collective-permute-start | bytes 344072 | tf_op jit(solution)/shard_map/ppermute | solution.py:562
  14.6 0.0 collective-permute-done.3.refs_2_
  14.6 0.0 collective-permute-start.4
  14.6 0.0 collective-permute-done.2.refs_1_
  14.6 0.5 %collective-permute-start.5 = (f32[176,128]{1,0:T(8,128)S(1)}, f32[176,128]{1,0:T(8,128)S(1)}, u32[]{:S(2)}, u32[]{:S(2)}) collective-permute-start(f32[176,128]{1,0:T(8,128)S(1)} %collective-permute-done.2.refs_1_), channel_id=1, source_target_pairs={{0,2},{1,3},{2,0},{3,1},{4,6},{5,7},{6,4},{7,5},{8,10},{9,11},{10,... | collective-permute-start | bytes 270344 | tf_op jit(solution)/shard_map/ppermute | solution.py:562
  15.1 1.5 %shard_map.57.refs_0_ = f32[192,6,8,128]{3,2,1,0:T(8,128)S(1)} custom-call(f32[2,8,128]{2,1,0:T(8,128)S(1)} %get-tuple-element.17.refs_0_, f32[2,8,128]{2,1,0:T(8,128)S(1)} %collective-permute-done.refs_1_, f32[256,128]{1,0:T(8,128)S(1)} %get-tuple-element.18.refs_0_.refs_2_, f32[256,128]{1,0:T(8,128)S(1)} %get-tuple-element.19.refs_1_.refs_3_, ...), custom_call_target="tpu_custom_call" | custom-call | flops 10000000 | bytes 5480448 | tf_op jit(solution)/shard_map/pallas_call | solution.py:538
  16.5 1.5 %shard_map.58.refs_1_ = f32[184,6,8,128]{3,2,1,0:T(8,128)S(1)} custom-call(f32[192,6,8,128]{3,2,1,0:T(8,128)S(1)} %shard_map.57.refs_0_, f32[176,128]{1,0:T(8,128)S(1)} %collective-permute-done.2.refs_1_, f32[176,128]{1,0:T(8,128)S(1)} %collective-permute-done.3.refs_2_), custom_call_target="tpu_custom_call" | custom-call | flops 10000000 | bytes 9420800 | tf_op jit(solution)/shard_map/pallas_call | solution.py:538
  18.0 0.0 collective-permute-done.4.refs_2_
  18.0 0.0 collective-permute-done.5.refs_3_
  18.0 0.6 %shard_map.59.refs_2_ = f32[62,6,8,128]{3,2,1,0:T(8,128)S(1)} custom-call(f32[192,6,8,128]{3,2,1,0:T(8,128)S(1)} %shard_map.57.refs_0_, f32[184,6,8,128]{3,2,1,0:T(8,128)S(1)} %shard_map.58.refs_1_, f32[176,128]{1,0:T(8,128)S(1)} %collective-permute-done.4.refs_2_, f32[176,128]{1,0:T(8,128)S(1)} %collective-permute-done.5.refs_3_, ...), custom_call_target="tpu_custom_call" | custom-call | flops 10000000 | bytes 11689984 | tf_op jit(solution)/shard_map/pallas_call | solution.py:538
  18.7 0.0 collective-permute-done.7.refs_7_
  18.7 0.6 %shard_map.60.refs_3_ = f32[62,6,8,128]{3,2,1,0:T(8,128)S(1)} custom-call(f32[192,6,8,128]{3,2,1,0:T(8,128)S(1)} %shard_map.57.refs_0_, f32[184,6,8,128]{3,2,1,0:T(8,128)S(1)} %shard_map.58.refs_1_, f32[176,128]{1,0:T(8,128)S(1)} %collective-permute-done.4.refs_2_, f32[176,128]{1,0:T(8,128)S(1)} %collective-permute-done.5.refs_3_, ...), custom_call_target="tpu_custom_call" | custom-call | flops 10000000 | bytes 12017664 | tf_op jit(solution)/shard_map/pallas_call | solution.py:538
  19.4 0.0 collective-permute-done.8.refs_4_
  19.4 1.0 %collective-permute-done.9.refs_5_ = f32[224,128]{1,0:T(8,128)S(1)} collective-permute-done((f32[224,128]{1,0:T(8,128)S(1)}, f32[224,128]{1,0:T(8,128)S(1)}, u32[]{:S(2)}, u32[]{:S(2)}) %collective-permute-start.9) | collective-permute-done | bytes 114720 | tf_op jit(solution)/shard_map/ppermute | solution.py:562
  20.4 1.0 %shard_map.61 = (f32[4,16,128]{2,1,0:T(8,128)S(1)}, f32[4,16,128]{2,1,0:T(8,128)S(1)}) custom-call(f32[192,6,8,128]{3,2,1,0:T(8,128)S(1)} %shard_map.57.refs_0_, f32[184,6,8,128]{3,2,1,0:T(8,128)S(1)} %shard_map.58.refs_1_, f32[62,6,8,128]{3,2,1,0:T(8,128)S(1)} %shard_map.59.refs_2_, f32[62,6,8,128]{3,2,1,0:T(8,128)S(1)} %shard_map.60.refs_3_, ...), custom_call_target="tpu_custom_call" | custom-call | flops 10000000 | bytes 12582912 | tf_op jit(solution)/shard_map/pallas_call | solution.py:538
  21.4 0.2 collective-permute-start.10
  21.6 1.1 %collective-permute-done.10.refs_1_ = f32[4,16,128]{2,1,0:T(8,128)S(1)} collective-permute-done((f32[4,16,128]{2,1,0:T(8,128)S(1)}, f32[4,16,128]{2,1,0:T(8,128)S(1)}, u32[]{:S(2)}, u32[]{:S(2)}) %collective-permute-start.10) | collective-permute-done | bytes 32800 | tf_op jit(solution)/shard_map/ppermute | solution.py:562
  22.7 0.6 %shard_map.62 = f32[128,128]{1,0:T(8,128)} custom-call(f32[4,16,128]{2,1,0:T(8,128)S(1)} %get-tuple-element.27.refs_0_, f32[4,16,128]{2,1,0:T(8,128)S(1)} %collective-permute-done.10.refs_1_), custom_call_target="tpu_custom_call" | custom-call | bytes 131072 | tf_op jit(solution)/shard_map/pallas_call | solution.py:538
  (3 shorter events, 0.0 us)
Async XLA Ops:
  1.3 8.0 %collective-permute-start.1 = (f32[944,128]{1,0:T(8,128)S(1)}, f32[944,128]{1,0:T(8,128)S(1)}, u32[]{:S(2)}, u32[]{:S(2)}) collective-permute-start(f32[944,128]{1,0:T(8,128)S(1)} %get-tuple-element.21), channel_id=1, source_target_pairs={{0,2},{1,3},{2,0},{3,1},{4,6},{5,7},{6,4},{7,5},{8,10},{9,11},{10,... | collective-permute-start | bytes 1449992 | tf_op jit(solution)/shard_map/ppermute | solution.py:562
  1.9 7.4 %collective-permute-start.6 = (f32[320,128]{1,0:T(8,128)S(1)}, f32[320,128]{1,0:T(8,128)S(1)}, u32[]{:S(2)}, u32[]{:S(2)}) collective-permute-start(f32[320,128]{1,0:T(8,128)S(1)} %get-tuple-element.24), channel_id=1, source_target_pairs={{0,1},{1,0},{2,3},{3,2},{4,5},{5,4},{6,7},{7,6},{8,9},{9,8},{10,11... | collective-permute-start | bytes 491528 | tf_op jit(solution)/shard_map/ppermute | solution.py:562
  4.4 6.8 %collective-permute-start = (f32[2,8,128]{2,1,0:T(8,128)S(1)}, f32[2,8,128]{2,1,0:T(8,128)S(1)}, u32[]{:S(2)}, u32[]{:S(2)}) collective-permute-start(f32[2,8,128]{2,1,0:T(8,128)S(1)} %get-tuple-element.17.refs_0_), channel_id=1, source_target_pairs={{0,1},{1,0},{2,3},{3,2},{4,5},{5,4},{6,7},{7,6},{8,9},{9,8},{10,11... | collective-permute-start | bytes 24584 | tf_op jit(solution)/shard_map/ppermute | solution.py:562
  4.5 10.1 %collective-permute-start.2 = (f32[176,128]{1,0:T(8,128)S(1)}, f32[176,128]{1,0:T(8,128)S(1)}, u32[]{:S(2)}, u32[]{:S(2)}) collective-permute-start(f32[176,128]{1,0:T(8,128)S(1)} %get-tuple-element.22), channel_id=1, source_target_pairs={{0,4},{1,5},{2,14},{3,15},{4,8},{5,9},{6,2},{7,3},{8,12},{9,13},{1... | collective-permute-start | bytes 270344 | tf_op jit(solution)/shard_map/ppermute | solution.py:562
  6.5 8.0 %collective-permute-start.3 = (f32[176,128]{1,0:T(8,128)S(1)}, f32[176,128]{1,0:T(8,128)S(1)}, u32[]{:S(2)}, u32[]{:S(2)}) collective-permute-start(f32[176,128]{1,0:T(8,128)S(1)} %get-tuple-element.23), channel_id=1, source_target_pairs={{0,14},{1,15},{2,4},{3,5},{4,2},{5,3},{6,8},{7,9},{8,6},{9,7},{10,... | collective-permute-start | bytes 270344 | tf_op jit(solution)/shard_map/ppermute | solution.py:562
  9.3 9.4 %collective-permute-start.7 = (f32[320,128]{1,0:T(8,128)S(1)}, f32[320,128]{1,0:T(8,128)S(1)}, u32[]{:S(2)}, u32[]{:S(2)}) collective-permute-start(f32[320,128]{1,0:T(8,128)S(1)} %collective-permute-done.6.refs_6_), channel_id=1, source_target_pairs={{0,2},{1,3},{2,0},{3,1},{4,6},{5,7},{6,4},{7,5},{8,10},{9,11},{10,... | collective-permute-start | bytes 491528 | tf_op jit(solution)/shard_map/ppermute | solution.py:562
  9.4 10.0 %collective-permute-start.8 = (f32[224,128]{1,0:T(8,128)S(1)}, f32[224,128]{1,0:T(8,128)S(1)}, u32[]{:S(2)}, u32[]{:S(2)}) collective-permute-start(f32[224,128]{1,0:T(8,128)S(1)} %pad_maximum_fusion), channel_id=1, source_target_pairs={{0,4},{1,5},{2,14},{3,15},{4,8},{5,9},{6,2},{7,3},{8,12},{9,13},{1... | collective-permute-start | bytes 344072 | tf_op jit(solution)/shard_map/ppermute | solution.py:562
  11.3 9.1 %collective-permute-start.9 = (f32[224,128]{1,0:T(8,128)S(1)}, f32[224,128]{1,0:T(8,128)S(1)}, u32[]{:S(2)}, u32[]{:S(2)}) collective-permute-start(f32[224,128]{1,0:T(8,128)S(1)} %pad_maximum_fusion.1), channel_id=1, source_target_pairs={{0,15},{1,14},{2,5},{3,4},{4,3},{5,2},{6,9},{7,8},{8,7},{9,6},{10,... | collective-permute-start | bytes 344072 | tf_op jit(solution)/shard_map/ppermute | solution.py:562
  14.6 3.5 %collective-permute-start.4 = (f32[176,128]{1,0:T(8,128)S(1)}, f32[176,128]{1,0:T(8,128)S(1)}, u32[]{:S(2)}, u32[]{:S(2)}) collective-permute-start(f32[176,128]{1,0:T(8,128)S(1)} %collective-permute-done.3.refs_2_), channel_id=1, source_target_pairs={{0,2},{1,3},{2,0},{3,1},{4,6},{5,7},{6,4},{7,5},{8,10},{9,11},{10,... | collective-permute-start | bytes 270344 | tf_op jit(solution)/shard_map/ppermute | solution.py:562
  14.6 3.5 %collective-permute-start.5 = (f32[176,128]{1,0:T(8,128)S(1)}, f32[176,128]{1,0:T(8,128)S(1)}, u32[]{:S(2)}, u32[]{:S(2)}) collective-permute-start(f32[176,128]{1,0:T(8,128)S(1)} %collective-permute-done.2.refs_1_), channel_id=1, source_target_pairs={{0,2},{1,3},{2,0},{3,1},{4,6},{5,7},{6,4},{7,5},{8,10},{9,11},{10,... | collective-permute-start | bytes 270344 | tf_op jit(solution)/shard_map/ppermute | solution.py:562
  21.4 1.3 %collective-permute-start.10 = (f32[4,16,128]{2,1,0:T(8,128)S(1)}, f32[4,16,128]{2,1,0:T(8,128)S(1)}, u32[]{:S(2)}, u32[]{:S(2)}) collective-permute-start(f32[4,16,128]{2,1,0:T(8,128)S(1)} %get-tuple-element.28), channel_id=1, source_target_pairs={{0,2},{1,3},{2,0},{3,1},{4,6},{5,7},{6,4},{7,5},{8,10},{9,11},{10,... | collective-permute-start | bytes 98312 | tf_op jit(solution)/shard_map/ppermute | solution.py:562
where the time goes:
time: 23.5 us; the launch traced here: 23.3 us
  starting transfers between devices  12.8 us (54%)
  Pallas kernels  7.19 us (31%)
  waiting for transfers between devices  3.24 us (14%)
    ppermute x11, starting transfers between devices, along(): return lax.ppermute(value, ('tx', 'ty', 'dose'), pairs)  12.8 us
    pallas_call x8, Pallas kernels, call(): pl.pallas_call(body, out_shape=tuple(outs), in_specs=[pl.BlockSpec(memory...  7.19 us
    ppermute x11, waiting for transfers between devices, along(): return lax.ppermute(value, ('tx', 'ty', 'dose'), pairs)  3.24 us
  transfers between devices with their start and end apart: 11, of which 3 were waited for; matrix products, arithmetic and copies ran while one was open for 0% of the time, Pallas kernels for 18%

commit v1 on v0

--- a/solution.py
+++ b/solution.py
@@ -472,38 +472,43 @@
         backward_rows(spread, past, back, d, table)
 
 
-def back_far_kernel(rows, window, local, near, far, *refs):
+def back_far_kernel(rows, window, local, group, near, far, back_near, sent, *refs):
     doses, groups = window.doses, window.groups
-    backs, refs = refs[:doses], refs[doses:]
-    sends = refs[:doses]
-    mine, other, store, full = refs[doses:]
-    layouts = halo_layouts(window, local)
+    sums, refs = (refs[0], refs[1:]) if group else (None, refs)
     half = rows // 2
     total = local * doses
     owner = lax.axis_index("dose")
+    layouts = halo_layouts(window, local)
     spread = make_spread()
     past = Fields(rows, (near, near_rows, 0, total), (far, far_rows, 0, total))
-    stores = [(ref, back_near_rows, k * local, local) for k, ref in enumerate(backs)]
-    back = Fields(rows, *stores, (store, back_far_rows, 0, total))
+    first, store = group * local, refs[-1] if group + 1 < doses else refs[-2]
+    back = Fields(rows, (back_near, back_near_rows, first, local), (store, back_far_rows, first, local))
     table = back_far_rows(rows)
-    for d in range(total):
-        k, i = divmod(d, local)
+    for i in range(local):
         for row in range(*table["ct"]):
             place = i * HALO_COT - 1 - row
-            value = layouts[0].get(sends[k], place, owner)
-            back.put("ct", d, row, value + layouts[1].get(sends[k], place, owner, layouts[0].size))
-        backward_rows(spread, past, back, d, table)
+            value = layouts[0].get(sent, place, owner)
+            value += layouts[1].get(sent, place, owner, layouts[0].size)
+            back.put("ct", first + i, row, value)
+        backward_rows(spread, past, back, first + i, table)
     for row in range(half):
-        value = back.get("g", 0, row)
-        for d in range(1, total):
-            value = [v + w for v, w in zip(value, back.get("g", d, row))]
+        value = back.get("g", first, row)
+        for i in range(1, local):
+            value = [v + w for v, w in zip(value, back.get("g", first + i, row))]
+        if group:
+            value = [v + sums[row, i] for i, v in enumerate(value)]
         for i in range(2 * groups):
-            side, k = divmod(i, groups)
-            full[side, row, pl.ds(k, SUB, stride=groups), :] = value[i]
-    start = pl.multiple_of(owner * window.piece - window.start(owner), SUB)
-    for side, out in enumerate((mine, other)):
-        for row in range(half):
-            out[row] = full[side, row, pl.ds(start, window.piece), :]
+            if group + 1 < doses:
+                refs[0][row, i] = value[i]
+            else:
+                side, k = divmod(i, groups)
+                refs[-1][side, row, pl.ds(k, SUB, stride=groups), :] = value[i]
+    if group + 1 == doses:
+        full = refs[-1]
+        start = pl.multiple_of(owner * window.piece - window.start(owner), SUB)
+        for side, out in enumerate(refs[:2]):
+            for row in range(half):
+                out[row] = full[side, row, pl.ds(start, window.piece), :]
 
 
 def join_kernel(rows, piece, mine, other, out):
@@ -617,17 +622,19 @@
             [array(*store(back_near_rows, local))],
             flops=10_000_000,
         )
-    mine, other = call(
-        back_far_kernel,
-        (rows, window, local),
-        [near, far] + backs + sends,
-        [array(half, piece)] * 2,
-        [
-            pltpu.VMEM(store(back_far_rows) + (lanes,), f32),
-            pltpu.VMEM((2, half, window.size, lanes), f32),
-        ],
-        flops=10_000_000,
-    )
+    sums = []
+    for k in range(doses):
+        final = k + 1 == doses
+        sums = call(
+            back_far_kernel,
+            (rows, window, local, k),
+            [near, far, backs[k], sends[k]] + list(sums),
+            [array(half, piece)] * 2 if final else [array(half, 2 * groups, SUB)],
+            [pltpu.VMEM(store(back_far_rows, local) + (lanes,), f32)]
+            + [pltpu.VMEM((2, half, window.size, lanes), f32)] * final,
+            flops=10_000_000,
+        )
+    mine, other = sums
     other = across(other)
     (out,) = call(join_kernel, (rows, piece), (mine, other), [array(piece * rows)])
     return out.reshape(piece, rows, lanes)

time: 23.5 us -> 23 us (0.979)
  waiting for transfers between devices: 3.24 us -> 2.61 us
    ppermute x11, waiting for transfers between devices: 3.24 us -> 2.61 us  [along(): return lax.ppermute(value, ('tx', 'ty', 'dose'), pairs)]
    pallas_call x8 -> x9, Pallas kernels: 7.19 us -> 7.31 us  [call(): pl.pallas_call(body, out_shape=tuple(outs), in_specs=[pl.BlockSpec(memory...]
  transfers between devices with their start and end apart: 11 -> 11, of which waited for: 3 -> 3; matrix products, arithmetic and copies ran while one was open for 0% -> 0% of each run, Pallas kernels for 18% -> 21%
where the time goes in v1:
time: 23 us; the launch traced here: 22.8 us
  starting transfers between devices  12.8 us (56%)
  Pallas kernels  7.31 us (32%)
  waiting for transfers between devices  2.61 us (11%)
    ppermute x11, starting transfers between devices, along(): return lax.ppermute(value, ('tx', 'ty', 'dose'), pairs)  12.8 us
    pallas_call x9, Pallas kernels, call(): pl.pallas_call(body, out_shape=tuple(outs), in_specs=[pl.BlockSpec(memory...  7.31 us
    ppermute x11, waiting for transfers between devices, along(): return lax.ppermute(value, ('tx', 'ty', 'dose'), pairs)  2.61 us
  transfers between devices with their start and end apart: 11, of which 3 were waited for; matrix products, arithmetic and copies ran while one was open for 0% of the time, Pallas kernels for 21%

profile of v1, /device:TPU:0, one launch (start us, length us, event | category | flops | bytes accessed | tf_op | source)
XLA Modules:
  0.0 22.8 jit_solution(8852907778579788069)
XLA Ops:
  0.0 1.1 %shard_map.55 = (f32[176,128]{1,0:T(8,128)S(1)}, f32[176,128]{1,0:T(8,128)S(1)}, f32[2,8,128]{2,1,0:T(8,128)S(1)}, f32[256,128]{1,0:T(8,128)S(1)}, f32[256,128]{1,0:T(8,128)S(1)}, /*index=5*/f32[512,128]{1,0:T(8,128)S(1)}) custom-call(f32[256,128]{1,0:T(8,128)} %bitcast.5, f32[256,128]{1,0:T(8,128)} %bitcast.6, f32[512,128]{1,0:T(8,128)} %bitcast.4, ...), custom_call_target="tpu_custom_call" | custom-call | bytes 1237064 | tf_op jit(solution)/shard_map/pallas_call | solution.py:543
  1.2 0.2 shard_map.56
  1.3 0.6 %collective-permute-start.1 = (f32[944,128]{1,0:T(8,128)S(1)}, f32[944,128]{1,0:T(8,128)S(1)}, u32[]{:S(2)}, u32[]{:S(2)}) collective-permute-start(f32[944,128]{1,0:T(8,128)S(1)} %get-tuple-element.21), channel_id=1, source_target_pairs={{0,2},{1,3},{2,0},{3,1},{4,6},{5,7},{6,4},{7,5},{8,10},{9,11},{10,... | collective-permute-start | bytes 1449992 | tf_op jit(solution)/shard_map/ppermute | solution.py:567
  1.9 2.6 %collective-permute-start.6 = (f32[320,128]{1,0:T(8,128)S(1)}, f32[320,128]{1,0:T(8,128)S(1)}, u32[]{:S(2)}, u32[]{:S(2)}) collective-permute-start(f32[320,128]{1,0:T(8,128)S(1)} %get-tuple-element.24), channel_id=1, source_target_pairs={{0,1},{1,0},{2,3},{3,2},{4,5},{5,4},{6,7},{7,6},{8,9},{9,8},{10,11... | collective-permute-start | bytes 491528 | tf_op jit(solution)/shard_map/ppermute | solution.py:567
  4.4 0.1 collective-permute-start
  4.5 2.0 %collective-permute-start.2 = (f32[176,128]{1,0:T(8,128)S(1)}, f32[176,128]{1,0:T(8,128)S(1)}, u32[]{:S(2)}, u32[]{:S(2)}) collective-permute-start(f32[176,128]{1,0:T(8,128)S(1)} %get-tuple-element.22), channel_id=1, source_target_pairs={{0,4},{1,5},{2,14},{3,15},{4,8},{5,9},{6,2},{7,3},{8,12},{9,13},{1... | collective-permute-start | bytes 270344 | tf_op jit(solution)/shard_map/ppermute | solution.py:567
  6.5 1.7 %collective-permute-start.3 = (f32[176,128]{1,0:T(8,128)S(1)}, f32[176,128]{1,0:T(8,128)S(1)}, u32[]{:S(2)}, u32[]{:S(2)}) collective-permute-start(f32[176,128]{1,0:T(8,128)S(1)} %get-tuple-element.23), channel_id=1, source_target_pairs={{0,14},{1,15},{2,4},{3,5},{4,2},{5,3},{6,8},{7,9},{8,6},{9,7},{10,... | collective-permute-start | bytes 270344 | tf_op jit(solution)/shard_map/ppermute | solution.py:567
  8.2 1.1 %collective-permute-done.6.refs_6_ = f32[320,128]{1,0:T(8,128)S(1)} collective-permute-done((f32[320,128]{1,0:T(8,128)S(1)}, f32[320,128]{1,0:T(8,128)S(1)}, u32[]{:S(2)}, u32[]{:S(2)}) %collective-permute-start.6) | collective-permute-done | bytes 163872 | tf_op jit(solution)/shard_map/ppermute | solution.py:567
  9.3 0.0 collective-permute-start.7
  9.3 0.0 collective-permute-done.1.refs_4_.refs_5_
  9.4 1.9 %collective-permute-start.9 = (f32[224,128]{1,0:T(8,128)S(1)}, f32[224,128]{1,0:T(8,128)S(1)}, u32[]{:S(2)}, u32[]{:S(2)}) collective-permute-start(f32[224,128]{1,0:T(8,128)S(1)} %pad_maximum_fusion.1), channel_id=1, source_target_pairs={{0,4},{1,5},{2,14},{3,15},{4,8},{5,9},{6,2},{7,3},{8,12},{9,13},{1... | collective-permute-start | bytes 344072 | tf_op jit(solution)/shard_map/ppermute | solution.py:567
  11.2 0.0 collective-permute-done.refs_1_
  11.3 3.3 %collective-permute-start.8 = (f32[224,128]{1,0:T(8,128)S(1)}, f32[224,128]{1,0:T(8,128)S(1)}, u32[]{:S(2)}, u32[]{:S(2)}) collective-permute-start(f32[224,128]{1,0:T(8,128)S(1)} %pad_maximum_fusion), channel_id=1, source_target_pairs={{0,15},{1,14},{2,5},{3,4},{4,3},{5,2},{6,9},{7,8},{8,7},{9,6},{10,... | collective-permute-start | bytes 344072 | tf_op jit(solution)/shard_map/ppermute | solution.py:567
  14.6 0.0 collective-permute-done.3.refs_2_
  14.6 0.0 collective-permute-start.4
  14.6 0.0 collective-permute-done.2.refs_1_
  14.6 0.5 %collective-permute-start.5 = (f32[176,128]{1,0:T(8,128)S(1)}, f32[176,128]{1,0:T(8,128)S(1)}, u32[]{:S(2)}, u32[]{:S(2)}) collective-permute-start(f32[176,128]{1,0:T(8,128)S(1)} %collective-permute-done.2.refs_1_), channel_id=1, source_target_pairs={{0,2},{1,3},{2,0},{3,1},{4,6},{5,7},{6,4},{7,5},{8,10},{9,11},{10,... | collective-permute-start | bytes 270344 | tf_op jit(solution)/shard_map/ppermute | solution.py:567
  15.1 1.5 %shard_map.57.refs_0_ = f32[192,6,8,128]{3,2,1,0:T(8,128)S(1)} custom-call(f32[2,8,128]{2,1,0:T(8,128)S(1)} %get-tuple-element.17.refs_0_, f32[2,8,128]{2,1,0:T(8,128)S(1)} %collective-permute-done.refs_1_, f32[256,128]{1,0:T(8,128)S(1)} %get-tuple-element.18.refs_0_.refs_2_, f32[256,128]{1,0:T(8,128)S(1)} %get-tuple-element.19.refs_1_.refs_3_, ...), custom_call_target="tpu_custom_call" | custom-call | flops 10000000 | bytes 5480448 | tf_op jit(solution)/shard_map/pallas_call | solution.py:543
  16.6 1.6 %shard_map.58.refs_1_ = f32[184,6,8,128]{3,2,1,0:T(8,128)S(1)} custom-call(f32[192,6,8,128]{3,2,1,0:T(8,128)S(1)} %shard_map.57.refs_0_, f32[176,128]{1,0:T(8,128)S(1)} %collective-permute-done.2.refs_1_, f32[176,128]{1,0:T(8,128)S(1)} %collective-permute-done.3.refs_2_), custom_call_target="tpu_custom_call" | custom-call | flops 10000000 | bytes 9420800 | tf_op jit(solution)/shard_map/pallas_call | solution.py:543
  18.2 0.0 collective-permute-done.4.refs_2_
  18.2 0.0 collective-permute-done.5.refs_3_
  18.2 0.6 %shard_map.60.refs_2_ = f32[62,6,8,128]{3,2,1,0:T(8,128)S(1)} custom-call(f32[192,6,8,128]{3,2,1,0:T(8,128)S(1)} %shard_map.57.refs_0_, f32[184,6,8,128]{3,2,1,0:T(8,128)S(1)} %shard_map.58.refs_1_, f32[176,128]{1,0:T(8,128)S(1)} %collective-permute-done.4.refs_2_, f32[176,128]{1,0:T(8,128)S(1)} %collective-permute-done.5.refs_3_, ...), custom_call_target="tpu_custom_call" | custom-call | flops 10000000 | bytes 11689984 | tf_op jit(solution)/shard_map/pallas_call | solution.py:543
  18.8 0.0 collective-permute-done.7.refs_7_
  18.8 0.6 %shard_map.59.refs_2_ = f32[62,6,8,128]{3,2,1,0:T(8,128)S(1)} custom-call(f32[192,6,8,128]{3,2,1,0:T(8,128)S(1)} %shard_map.57.refs_0_, f32[184,6,8,128]{3,2,1,0:T(8,128)S(1)} %shard_map.58.refs_1_, f32[176,128]{1,0:T(8,128)S(1)} %collective-permute-done.4.refs_2_, f32[176,128]{1,0:T(8,128)S(1)} %collective-permute-done.5.refs_3_, ...), custom_call_target="tpu_custom_call" | custom-call | flops 10000000 | bytes 12017664 | tf_op jit(solution)/shard_map/pallas_call | solution.py:543
  19.4 0.0 collective-permute-done.9.refs_3_
  19.5 0.5 %shard_map.61.refs_4_ = f32[4,6,8,128]{3,2,1,0:T(8,128)S(1)} custom-call(f32[192,6,8,128]{3,2,1,0:T(8,128)S(1)} %shard_map.57.refs_0_, f32[184,6,8,128]{3,2,1,0:T(8,128)S(1)} %shard_map.58.refs_1_, f32[62,6,8,128]{3,2,1,0:T(8,128)S(1)} %shard_map.60.refs_2_, f32[224,128]{1,0:T(8,128)S(1)} %collective-permute-done.9.refs_3_), custom_call_target="tpu_custom_call" | custom-call | flops 10000000 | bytes 10977280 | tf_op jit(solution)/shard_map/pallas_call | solution.py:543
  20.0 0.4 %collective-permute-done.8.refs_3_ = f32[224,128]{1,0:T(8,128)S(1)} collective-permute-done((f32[224,128]{1,0:T(8,128)S(1)}, f32[224,128]{1,0:T(8,128)S(1)}, u32[]{:S(2)}, u32[]{:S(2)}) %collective-permute-start.8) | collective-permute-done | bytes 114720 | tf_op jit(solution)/shard_map/ppermute | solution.py:567
  20.4 0.5 %shard_map.62 = (f32[4,16,128]{2,1,0:T(8,128)S(1)}, f32[4,16,128]{2,1,0:T(8,128)S(1)}) custom-call(f32[192,6,8,128]{3,2,1,0:T(8,128)S(1)} %shard_map.57.refs_0_, f32[184,6,8,128]{3,2,1,0:T(8,128)S(1)} %shard_map.58.refs_1_, f32[62,6,8,128]{3,2,1,0:T(8,128)S(1)} %shard_map.59.refs_2_, f32[224,128]{1,0:T(8,128)S(1)} %collective-permute-done.8.refs_3_, ...), custom_call_target="tpu_custom_call" | custom-call | flops 10000000 | bytes 11042816 | tf_op jit(solution)/shard_map/pallas_call | solution.py:543
  20.9 0.2 collective-permute-start.10
  21.1 1.1 %collective-permute-done.10.refs_1_ = f32[4,16,128]{2,1,0:T(8,128)S(1)} collective-permute-done((f32[4,16,128]{2,1,0:T(8,128)S(1)}, f32[4,16,128]{2,1,0:T(8,128)S(1)}, u32[]{:S(2)}, u32[]{:S(2)}) %collective-permute-start.10) | collective-permute-done | bytes 32800 | tf_op jit(solution)/shard_map/ppermute | solution.py:567
  22.2 0.6 %shard_map.63 = f32[128,128]{1,0:T(8,128)} custom-call(f32[4,16,128]{2,1,0:T(8,128)S(1)} %get-tuple-element.27.refs_0_, f32[4,16,128]{2,1,0:T(8,128)S(1)} %collective-permute-done.10.refs_1_), custom_call_target="tpu_custom_call" | custom-call | bytes 131072 | tf_op jit(solution)/shard_map/pallas_call | solution.py:543
  (3 shorter events, 0.0 us)
Async XLA Ops:
  1.3 8.0 %collective-permute-start.1 = (f32[944,128]{1,0:T(8,128)S(1)}, f32[944,128]{1,0:T(8,128)S(1)}, u32[]{:S(2)}, u32[]{:S(2)}) collective-permute-start(f32[944,128]{1,0:T(8,128)S(1)} %get-tuple-element.21), channel_id=1, source_target_pairs={{0,2},{1,3},{2,0},{3,1},{4,6},{5,7},{6,4},{7,5},{8,10},{9,11},{10,... | collective-permute-start | bytes 1449992 | tf_op jit(solution)/shard_map/ppermute | solution.py:567
  1.9 7.4 %collective-permute-start.6 = (f32[320,128]{1,0:T(8,128)S(1)}, f32[320,128]{1,0:T(8,128)S(1)}, u32[]{:S(2)}, u32[]{:S(2)}) collective-permute-start(f32[320,128]{1,0:T(8,128)S(1)} %get-tuple-element.24), channel_id=1, source_target_pairs={{0,1},{1,0},{2,3},{3,2},{4,5},{5,4},{6,7},{7,6},{8,9},{9,8},{10,11... | collective-permute-start | bytes 491528 | tf_op jit(solution)/shard_map/ppermute | solution.py:567
  4.4 6.8 %collective-permute-start = (f32[2,8,128]{2,1,0:T(8,128)S(1)}, f32[2,8,128]{2,1,0:T(8,128)S(1)}, u32[]{:S(2)}, u32[]{:S(2)}) collective-permute-start(f32[2,8,128]{2,1,0:T(8,128)S(1)} %get-tuple-element.17.refs_0_), channel_id=1, source_target_pairs={{0,1},{1,0},{2,3},{3,2},{4,5},{5,4},{6,7},{7,6},{8,9},{9,8},{10,11... | collective-permute-start | bytes 24584 | tf_op jit(solution)/shard_map/ppermute | solution.py:567
  4.5 10.1 %collective-permute-start.2 = (f32[176,128]{1,0:T(8,128)S(1)}, f32[176,128]{1,0:T(8,128)S(1)}, u32[]{:S(2)}, u32[]{:S(2)}) collective-permute-start(f32[176,128]{1,0:T(8,128)S(1)} %get-tuple-element.22), channel_id=1, source_target_pairs={{0,4},{1,5},{2,14},{3,15},{4,8},{5,9},{6,2},{7,3},{8,12},{9,13},{1... | collective-permute-start | bytes 270344 | tf_op jit(solution)/shard_map/ppermute | solution.py:567
  6.5 8.0 %collective-permute-start.3 = (f32[176,128]{1,0:T(8,128)S(1)}, f32[176,128]{1,0:T(8,128)S(1)}, u32[]{:S(2)}, u32[]{:S(2)}) collective-permute-start(f32[176,128]{1,0:T(8,128)S(1)} %get-tuple-element.23), channel_id=1, source_target_pairs={{0,14},{1,15},{2,4},{3,5},{4,2},{5,3},{6,8},{7,9},{8,6},{9,7},{10,... | collective-permute-start | bytes 270344 | tf_op jit(solution)/shard_map/ppermute | solution.py:567
  9.3 9.5 %collective-permute-start.7 = (f32[320,128]{1,0:T(8,128)S(1)}, f32[320,128]{1,0:T(8,128)S(1)}, u32[]{:S(2)}, u32[]{:S(2)}) collective-permute-start(f32[320,128]{1,0:T(8,128)S(1)} %collective-permute-done.6.refs_6_), channel_id=1, source_target_pairs={{0,2},{1,3},{2,0},{3,1},{4,6},{5,7},{6,4},{7,5},{8,10},{9,11},{10,... | collective-permute-start | bytes 491528 | tf_op jit(solution)/shard_map/ppermute | solution.py:567
  9.4 10.1 %collective-permute-start.9 = (f32[224,128]{1,0:T(8,128)S(1)}, f32[224,128]{1,0:T(8,128)S(1)}, u32[]{:S(2)}, u32[]{:S(2)}) collective-permute-start(f32[224,128]{1,0:T(8,128)S(1)} %pad_maximum_fusion.1), channel_id=1, source_target_pairs={{0,4},{1,5},{2,14},{3,15},{4,8},{5,9},{6,2},{7,3},{8,12},{9,13},{1... | collective-permute-start | bytes 344072 | tf_op jit(solution)/shard_map/ppermute | solution.py:567
  11.3 9.1 %collective-permute-start.8 = (f32[224,128]{1,0:T(8,128)S(1)}, f32[224,128]{1,0:T(8,128)S(1)}, u32[]{:S(2)}, u32[]{:S(2)}) collective-permute-start(f32[224,128]{1,0:T(8,128)S(1)} %pad_maximum_fusion), channel_id=1, source_target_pairs={{0,15},{1,14},{2,5},{3,4},{4,3},{5,2},{6,9},{7,8},{8,7},{9,6},{10,... | collective-permute-start | bytes 344072 | tf_op jit(solution)/shard_map/ppermute | solution.py:567
  14.6 3.6 %collective-permute-start.4 = (f32[176,128]{1,0:T(8,128)S(1)}, f32[176,128]{1,0:T(8,128)S(1)}, u32[]{:S(2)}, u32[]{:S(2)}) collective-permute-start(f32[176,128]{1,0:T(8,128)S(1)} %collective-permute-done.3.refs_2_), channel_id=1, source_target_pairs={{0,2},{1,3},{2,0},{3,1},{4,6},{5,7},{6,4},{7,5},{8,10},{9,11},{10,... | collective-permute-start | bytes 270344 | tf_op jit(solution)/shard_map/ppermute | solution.py:567
  14.6 3.6 %collective-permute-start.5 = (f32[176,128]{1,0:T(8,128)S(1)}, f32[176,128]{1,0:T(8,128)S(1)}, u32[]{:S(2)}, u32[]{:S(2)}) collective-permute-start(f32[176,128]{1,0:T(8,128)S(1)} %collective-permute-done.2.refs_1_), channel_id=1, source_target_pairs={{0,2},{1,3},{2,0},{3,1},{4,6},{5,7},{6,4},{7,5},{8,10},{9,11},{10,... | collective-permute-start | bytes 270344 | tf_op jit(solution)/shard_map/ppermute | solution.py:567
  20.9 1.3 %collective-permute-start.10 = (f32[4,16,128]{2,1,0:T(8,128)S(1)}, f32[4,16,128]{2,1,0:T(8,128)S(1)}, u32[]{:S(2)}, u32[]{:S(2)}) collective-permute-start(f32[4,16,128]{2,1,0:T(8,128)S(1)} %get-tuple-element.28), channel_id=1, source_target_pairs={{0,2},{1,3},{2,0},{3,1},{4,6},{5,7},{6,4},{7,5},{8,10},{9,11},{10,... | collective-permute-start | bytes 98312 | tf_op jit(solution)/shard_map/ppermute | solution.py:567

commit v2 on v1

--- a/solution.py
+++ b/solution.py
@@ -137,7 +137,7 @@
     return [swap[pl.ds((place * groups + k) * SUB, SUB), :] for k in range(groups)]
 
 
-def rest_kernel(rows, window, local, aerial, quench, cot, swap, *dense):
+def rest_kernel(rows, window, local, dose, aerial, quench, cot, swap, *dense):
     depth, groups, doses = window.depth, window.groups, window.doses
     area = rows * depth
     inner = rows // 2 + HALO_COT
@@ -169,6 +169,7 @@
             for d in range(local):
                 for row in range(rows):
                     whole.put(ref, d * rows + row, cot, d * area, rows, row, target)
+                ref[pl.ds(whole.size + d * SUB, SUB), :] = dose[d]
     place = 0
     parts = [(aerial, 0, rows), (quench, 0, rows)] + [(cot, d * area, inner) for d in range(local)]
     start = window.start(owner)
@@ -354,13 +355,11 @@
             fields.put("c%d" % n, d, row, value)
 
 
-def near_kernel(rows, window, local, *refs):
-    doses, groups = window.doses, window.groups
-    dose_refs, (aerial, quench, swap, near) = refs[:doses], refs[doses:]
+def near_kernel(rows, window, local, group, dose_ref, aerial, quench, swap, near):
+    groups = window.groups
     half = rows // 2
     spread = make_spread()
-    total = local * doses
-    fields = Fields(rows, (near, near_rows, 0, total))
+    fields = Fields(rows, (near, near_rows, 0, local))
     start = window.start(lax.axis_index("dose"))
 
     def source(raw, at, row):
@@ -369,8 +368,9 @@
 
     for row in range(rows):
         fields.put("q0", 0, row, [neutral_rate * v for v in source(quench, rows, row)])
-    for d in range(total):
-        dose = dose_refs[d // local][d % local]
+    size = whole_layout(rows, window, local).size
+    for d in range(local):
+        dose = dose_ref[pl.ds(size + d * SUB, SUB), :] if group else dose_ref[d]
         fields.put("dose", d, 0, [dose] * (2 * groups))
         rate = -exposure_rate * dose
         for row in range(rows):
@@ -381,9 +381,9 @@
         forward_rows(spread, fields, d, near_rows(rows))
 
 
-def far_kernel(rows, window, total, near, image_s, image_c, far):
+def far_kernel(rows, window, local, near, image_s, image_c, far):
     spread = make_spread()
-    fields = Fields(rows, (near, near_rows, 0, total), (far, far_rows, 0, total))
+    fields = Fields(rows, (near, near_rows, 0, local), (far, far_rows, 0, local))
     table = dict(far_rows(rows), e=(0, 0))
     owner = lax.axis_index("dose")
     layout = image_layout(window)
@@ -393,7 +393,7 @@
 
     for row in range(-HALO_QUENCH, 0):
         fields.put("q0", 0, row, [neutral_rate * v for v in source(HALO_AERIAL + HALO_QUENCH + row)])
-    for d in range(total):
+    for d in range(local):
         rate = -exposure_rate * fields.get("dose", d, 0)[0]
         for row in range(-HALO_AERIAL, 0):
             absorbed = [jnp.exp(rate * v) for v in source(-1 - row)]
@@ -435,19 +435,18 @@
 
 
 def back_near_kernel(rows, window, local, group, near, far, extra_own, extra_par, cot, swap, *refs):
-    doses, groups = window.doses, window.groups
+    groups = window.groups
     wholes, back_near = refs[:-1], refs[-1]
     half = rows // 2
     area = rows * window.depth
     inner = half + HALO_COT
-    total = local * doses
     spread = make_spread()
     owner = lax.axis_index("dose")
     start = window.start(owner)
     image = image_layout(window)
     whole = whole_layout(rows, window, local)
     for d in range(group * local, (group + 1) * local):
-        past = Fields(rows, (near, near_rows, 0, total), (far, far_rows, 0, total))
+        past = Fields(rows, (near, near_rows, group * local, local), (far, far_rows, group * local, local))
         rate = -exposure_rate * past.get("dose", d, 0)[0]
         light = [v for src in (extra_own, extra_par) for v in image.get(src, 0, owner)]
         past.more["a0", d, rows] = [neutral_rate - neutral_rate * jnp.exp(rate * v) for v in light]
@@ -476,11 +475,10 @@
     doses, groups = window.doses, window.groups
     sums, refs = (refs[0], refs[1:]) if group else (None, refs)
     half = rows // 2
-    total = local * doses
     owner = lax.axis_index("dose")
     layouts = halo_layouts(window, local)
     spread = make_spread()
-    past = Fields(rows, (near, near_rows, 0, total), (far, far_rows, 0, total))
+    past = Fields(rows, (near, near_rows, group * local, local), (far, far_rows, group * local, local))
     first, store = group * local, refs[-1] if group + 1 < doses else refs[-2]
     back = Fields(rows, (back_near, back_near_rows, first, local), (store, back_far_rows, first, local))
     table = back_far_rows(rows)
@@ -529,7 +527,6 @@
     assert rows == half + HALO_QUENCH and HALO_AERIAL == HALO_QUENCH + 1
     window = Window(depth, doses)
     groups, piece = window.groups, window.piece
-    total = local * doses
     f32 = jnp.float32
     aerial = aerial_image.reshape(depth * rows, lanes)
     quench = quencher.reshape(depth * rows, lanes)
@@ -553,8 +550,8 @@
     def array(*shape):
         return jax.ShapeDtypeStruct(shape + (lanes,), f32)
 
-    def store(table, count=total):
-        return (places_of(table(rows), count)[1], 2 * groups, SUB)
+    def store(table):
+        return (places_of(table(rows), local)[1], 2 * groups, SUB)
 
     def along(value, cross=0, step=1, k=0):
         pairs = []
@@ -571,7 +568,7 @@
 
     images = array(image_layout(window).size)
     handed, halo = swap_layout(rows, window, local)
-    whole = array(whole_layout(rows, window, local).size)
+    whole = array(whole_layout(rows, window, local).size + local * SUB)
     flat = [jax.ShapeDtypeStruct(x.shape, f32) for x in (aerial, quench, cot)]
     image_s, image_c, dose, aerial, quench, cot = call(
         image_kernel,
@@ -590,14 +587,14 @@
     rest = call(
         rest_kernel,
         (rows, window, local),
-        (aerial, quench, cot),
+        (dose, aerial, quench, cot),
         [array(handed + doses * halo)] + [array(halo)] * doses + [whole] * (doses - 1),
     )
     swap = across(rest[0])
     values, wholes = [dose], []
     for k in range(1, doses):
         arrived = along(rest[doses + k], step=0, k=k)
-        values.append(along(dose, step=0, k=k))
+        values.append(arrived)
         wholes.append([arrived, across(arrived)])
     sends = []
     for k in range(doses):
@@ -605,21 +602,27 @@
         both = jnp.concatenate((other, rest[1 + k]) if crosses(k) else (rest[1 + k], other), axis=0)
         sends.append(along(both, cross=int(crosses(k)), k=k))
 
-    (near,) = call(
-        near_kernel, (rows, window, local), values + [aerial, quench, swap], [array(*store(near_rows))], flops=10_000_000
-    )
     extra_own = across(image_c)
     extra_par = across(image_s)
-    (far,) = call(
-        far_kernel, (rows, window, total), (near, image_s, image_c), [array(*store(far_rows))], flops=10_000_000
-    )
+    nears, fars = [], []
+    for k in range(doses):
+        nears += call(
+            near_kernel,
+            (rows, window, local, k),
+            (values[k], aerial, quench, swap),
+            [array(*store(near_rows))],
+            flops=5_000_000,
+        )
+        fars += call(
+            far_kernel, (rows, window, local), (nears[k], image_s, image_c), [array(*store(far_rows))], flops=5_000_000
+        )
     backs = []
     for k in range(doses):
         backs += call(
             back_near_kernel,
             (rows, window, local, k),
-            [near, far, extra_own, extra_par, cot, swap] + (wholes[k - 1] if k else []),
-            [array(*store(back_near_rows, local))],
+            [nears[k], fars[k], extra_own, extra_par, cot, swap] + (wholes[k - 1] if k else []),
+            [array(*store(back_near_rows))],
             flops=10_000_000,
         )
     sums = []
@@ -628,9 +631,9 @@
         sums = call(
             back_far_kernel,
             (rows, window, local, k),
-            [near, far, backs[k], sends[k]] + list(sums),
+            [nears[k], fars[k], backs[k], sends[k]] + list(sums),
             [array(half, piece)] * 2 if final else [array(half, 2 * groups, SUB)],
-            [pltpu.VMEM(store(back_far_rows, local) + (lanes,), f32)]
+            [pltpu.VMEM(store(back_far_rows) + (lanes,), f32)]
             + [pltpu.VMEM((2, half, window.size, lanes), f32)] * final,
             flops=10_000_000,
         )

time: 23 us -> 23 us (level)
  starting transfers between devices: 12.8 us -> 12.5 us
  Pallas kernels: 7.31 us -> 7.56 us
    pallas_call x9 -> x11, Pallas kernels: 7.31 us -> 7.56 us  [call(): pl.pallas_call(body, out_shape=tuple(outs), in_specs=[pl.BlockSpec(memory...]
    ppermute x11 -> x10, starting transfers between devices: 12.8 us -> 12.5 us  [along(): return lax.ppermute(value, ('tx', 'ty', 'dose'), pairs)]
    ppermute x11 -> x10, waiting for transfers between devices: 2.61 us -> 2.71 us  [along(): return lax.ppermute(value, ('tx', 'ty', 'dose'), pairs)]
  transfers between devices with their start and end apart: 11 -> 10, of which waited for: 3 -> 3; matrix products, arithmetic and copies ran while one was open for 0% -> 0% of each run, Pallas kernels for 21% -> 22%
where the time goes in v2:
time: 23 us; the launch traced here: 22.9 us
  starting transfers between devices  12.5 us (54%)
  Pallas kernels  7.56 us (33%)
  waiting for transfers between devices  2.71 us (12%)
    ppermute x10, starting transfers between devices, along(): return lax.ppermute(value, ('tx', 'ty', 'dose'), pairs)  12.5 us
    pallas_call x11, Pallas kernels, call(): pl.pallas_call(body, out_shape=tuple(outs), in_specs=[pl.BlockSpec(memory...  7.56 us
    ppermute x10, waiting for transfers between devices, along(): return lax.ppermute(value, ('tx', 'ty', 'dose'), pairs)  2.71 us
  transfers between devices with their start and end apart: 10, of which 3 were waited for; matrix products, arithmetic and copies ran while one was open for 0% of the time, Pallas kernels for 22%

profile of v2, /device:TPU:0, one launch (start us, length us, event | category | flops | bytes accessed | tf_op | source)
XLA Modules:
  0.0 22.9 jit_solution(11103533019140094153)
XLA Ops:
  0.0 1.1 %shard_map.55 = (f32[176,128]{1,0:T(8,128)S(1)}, f32[176,128]{1,0:T(8,128)S(1)}, f32[2,8,128]{2,1,0:T(8,128)S(1)}, f32[256,128]{1,0:T(8,128)S(1)}, f32[256,128]{1,0:T(8,128)S(1)}, /*index=5*/f32[512,128]{1,0:T(8,128)S(1)}) custom-call(f32[256,128]{1,0:T(8,128)} %bitcast.5, f32[256,128]{1,0:T(8,128)} %bitcast.6, f32[512,128]{1,0:T(8,128)} %bitcast.4, ...), custom_call_target="tpu_custom_call" | custom-call | bytes 1237064 | tf_op jit(solution)/shard_map/pallas_call | solution.py:540
  1.2 0.2 shard_map.56
  1.3 0.6 %collective-permute-start.1 = (f32[944,128]{1,0:T(8,128)S(1)}, f32[944,128]{1,0:T(8,128)S(1)}, u32[]{:S(2)}, u32[]{:S(2)}) collective-permute-start(f32[944,128]{1,0:T(8,128)S(1)} %get-tuple-element.22), channel_id=1, source_target_pairs={{0,2},{1,3},{2,0},{3,1},{4,6},{5,7},{6,4},{7,5},{8,10},{9,11},{10,... | collective-permute-start | bytes 1449992 | tf_op jit(solution)/shard_map/ppermute | solution.py:564
  1.9 2.6 %collective-permute-start = (f32[336,128]{1,0:T(8,128)S(1)}, f32[336,128]{1,0:T(8,128)S(1)}, u32[]{:S(2)}, u32[]{:S(2)}) collective-permute-start(f32[336,128]{1,0:T(8,128)S(1)} %get-tuple-element.21), channel_id=1, source_target_pairs={{0,1},{1,0},{2,3},{3,2},{4,5},{5,4},{6,7},{7,6},{8,9},{9,8},{10,11... | collective-permute-start | bytes 516104 | tf_op jit(solution)/shard_map/ppermute | solution.py:564
  4.4 1.6 %collective-permute-start.2 = (f32[176,128]{1,0:T(8,128)S(1)}, f32[176,128]{1,0:T(8,128)S(1)}, u32[]{:S(2)}, u32[]{:S(2)}) collective-permute-start(f32[176,128]{1,0:T(8,128)S(1)} %get-tuple-element.23), channel_id=1, source_target_pairs={{0,4},{1,5},{2,14},{3,15},{4,8},{5,9},{6,2},{7,3},{8,12},{9,13},{1... | collective-permute-start | bytes 270344 | tf_op jit(solution)/shard_map/ppermute | solution.py:564
  6.0 2.0 %collective-permute-start.3 = (f32[176,128]{1,0:T(8,128)S(1)}, f32[176,128]{1,0:T(8,128)S(1)}, u32[]{:S(2)}, u32[]{:S(2)}) collective-permute-start(f32[176,128]{1,0:T(8,128)S(1)} %get-tuple-element.24), channel_id=1, source_target_pairs={{0,14},{1,15},{2,4},{3,5},{4,2},{5,3},{6,8},{7,9},{8,6},{9,7},{10,... | collective-permute-start | bytes 270344 | tf_op jit(solution)/shard_map/ppermute | solution.py:564
  8.0 1.4 %collective-permute-done.refs_0_.refs_6_ = f32[336,128]{1,0:T(8,128)S(1)} collective-permute-done((f32[336,128]{1,0:T(8,128)S(1)}, f32[336,128]{1,0:T(8,128)S(1)}, u32[]{:S(2)}, u32[]{:S(2)}) %collective-permute-start) | collective-permute-done | bytes 172064 | tf_op jit(solution)/shard_map/ppermute | solution.py:564
  9.4 0.0 collective-permute-start.6
  9.4 0.0 collective-permute-done.1.refs_3_.refs_5_
  9.4 1.9 %collective-permute-start.8 = (f32[224,128]{1,0:T(8,128)S(1)}, f32[224,128]{1,0:T(8,128)S(1)}, u32[]{:S(2)}, u32[]{:S(2)}) collective-permute-start(f32[224,128]{1,0:T(8,128)S(1)} %pad_maximum_fusion.1), channel_id=1, source_target_pairs={{0,4},{1,5},{2,14},{3,15},{4,8},{5,9},{6,2},{7,3},{8,12},{9,13},{1... | collective-permute-start | bytes 344072 | tf_op jit(solution)/shard_map/ppermute | solution.py:564
  11.3 3.3 %collective-permute-start.7 = (f32[224,128]{1,0:T(8,128)S(1)}, f32[224,128]{1,0:T(8,128)S(1)}, u32[]{:S(2)}, u32[]{:S(2)}) collective-permute-start(f32[224,128]{1,0:T(8,128)S(1)} %pad_maximum_fusion), channel_id=1, source_target_pairs={{0,15},{1,14},{2,5},{3,4},{4,3},{5,2},{6,9},{7,8},{8,7},{9,6},{10,... | collective-permute-start | bytes 344072 | tf_op jit(solution)/shard_map/ppermute | solution.py:564
  14.6 0.0 collective-permute-done.3.refs_2_
  14.6 0.0 collective-permute-start.4
  14.6 0.0 collective-permute-done.2.refs_1_
  14.6 0.5 %collective-permute-start.5 = (f32[176,128]{1,0:T(8,128)S(1)}, f32[176,128]{1,0:T(8,128)S(1)}, u32[]{:S(2)}, u32[]{:S(2)}) collective-permute-start(f32[176,128]{1,0:T(8,128)S(1)} %collective-permute-done.2.refs_1_), channel_id=1, source_target_pairs={{0,2},{1,3},{2,0},{3,1},{4,6},{5,7},{6,4},{7,5},{8,10},{9,11},{10,... | collective-permute-start | bytes 270344 | tf_op jit(solution)/shard_map/ppermute | solution.py:564
  15.2 0.8 %shard_map.60.refs_0_ = f32[100,6,8,128]{3,2,1,0:T(8,128)S(1)} custom-call(f32[2,8,128]{2,1,0:T(8,128)S(1)} %get-tuple-element.17.refs_0_, f32[256,128]{1,0:T(8,128)S(1)} %get-tuple-element.18.refs_1_, f32[256,128]{1,0:T(8,128)S(1)} %get-tuple-element.19.refs_2_, f32[944,128]{1,0:T(8,128)S(1)} %collective-permute-done.1.refs_3_.refs_5_), custom_call_target="tpu_custom_call" | custom-call | flops 5000000 | bytes 3211264 | tf_op jit(solution)/shard_map/pallas_call | solution.py:540
  16.0 0.8 %shard_map.57.refs_0_ = f32[100,6,8,128]{3,2,1,0:T(8,128)S(1)} custom-call(f32[336,128]{1,0:T(8,128)S(1)} %collective-permute-done.refs_0_.refs_6_, f32[256,128]{1,0:T(8,128)S(1)} %get-tuple-element.18.refs_1_, f32[256,128]{1,0:T(8,128)S(1)} %get-tuple-element.19.refs_2_, f32[944,128]{1,0:T(8,128)S(1)} %collective-permute-done.1.refs_3_.refs_5_), custom_call_target="tpu_custom_call" | custom-call | flops 5000000 | bytes 3375104 | tf_op jit(solution)/shard_map/pallas_call | solution.py:540
  16.8 0.8 %shard_map.61.refs_1_ = f32[94,6,8,128]{3,2,1,0:T(8,128)S(1)} custom-call(f32[100,6,8,128]{3,2,1,0:T(8,128)S(1)} %shard_map.60.refs_0_, f32[176,128]{1,0:T(8,128)S(1)} %collective-permute-done.2.refs_1_, f32[176,128]{1,0:T(8,128)S(1)} %collective-permute-done.3.refs_2_), custom_call_target="tpu_custom_call" | custom-call | flops 5000000 | bytes 4947968 | tf_op jit(solution)/shard_map/pallas_call | solution.py:540
  17.6 0.8 %shard_map.58.refs_1_ = f32[94,6,8,128]{3,2,1,0:T(8,128)S(1)} custom-call(f32[100,6,8,128]{3,2,1,0:T(8,128)S(1)} %shard_map.57.refs_0_, f32[176,128]{1,0:T(8,128)S(1)} %collective-permute-done.2.refs_1_, f32[176,128]{1,0:T(8,128)S(1)} %collective-permute-done.3.refs_2_), custom_call_target="tpu_custom_call" | custom-call | flops 5000000 | bytes 4947968 | tf_op jit(solution)/shard_map/pallas_call | solution.py:540
  18.5 0.0 collective-permute-done.4.refs_2_
  18.5 0.0 collective-permute-done.5.refs_3_
  18.5 0.6 %shard_map.62.refs_2_ = f32[62,6,8,128]{3,2,1,0:T(8,128)S(1)} custom-call(f32[100,6,8,128]{3,2,1,0:T(8,128)S(1)} %shard_map.60.refs_0_, f32[94,6,8,128]{3,2,1,0:T(8,128)S(1)} %shard_map.61.refs_1_, f32[176,128]{1,0:T(8,128)S(1)} %collective-permute-done.4.refs_2_, f32[176,128]{1,0:T(8,128)S(1)} %collective-permute-done.5.refs_3_, ...), custom_call_target="tpu_custom_call" | custom-call | flops 10000000 | bytes 7217152 | tf_op jit(solution)/shard_map/pallas_call | solution.py:540
  19.1 0.0 collective-permute-done.6.refs_7_
  19.1 0.6 %shard_map.59.refs_2_ = f32[62,6,8,128]{3,2,1,0:T(8,128)S(1)} custom-call(f32[100,6,8,128]{3,2,1,0:T(8,128)S(1)} %shard_map.57.refs_0_, f32[94,6,8,128]{3,2,1,0:T(8,128)S(1)} %shard_map.58.refs_1_, f32[176,128]{1,0:T(8,128)S(1)} %collective-permute-done.4.refs_2_, f32[176,128]{1,0:T(8,128)S(1)} %collective-permute-done.5.refs_3_, ...), custom_call_target="tpu_custom_call" | custom-call | flops 10000000 | bytes 7561216 | tf_op jit(solution)/shard_map/pallas_call | solution.py:540
  19.8 0.0 collective-permute-done.8.refs_3_
  19.8 0.5 %shard_map.63.refs_4_ = f32[4,6,8,128]{3,2,1,0:T(8,128)S(1)} custom-call(f32[100,6,8,128]{3,2,1,0:T(8,128)S(1)} %shard_map.60.refs_0_, f32[94,6,8,128]{3,2,1,0:T(8,128)S(1)} %shard_map.61.refs_1_, f32[62,6,8,128]{3,2,1,0:T(8,128)S(1)} %shard_map.62.refs_2_, f32[224,128]{1,0:T(8,128)S(1)} %collective-permute-done.8.refs_3_), custom_call_target="tpu_custom_call" | custom-call | flops 10000000 | bytes 6504448 | tf_op jit(solution)/shard_map/pallas_call | solution.py:540
  20.3 0.2 collective-permute-done.7.refs_3_
  20.5 0.5 %shard_map.64 = (f32[4,16,128]{2,1,0:T(8,128)S(1)}, f32[4,16,128]{2,1,0:T(8,128)S(1)}) custom-call(f32[100,6,8,128]{3,2,1,0:T(8,128)S(1)} %shard_map.57.refs_0_, f32[94,6,8,128]{3,2,1,0:T(8,128)S(1)} %shard_map.58.refs_1_, f32[62,6,8,128]{3,2,1,0:T(8,128)S(1)} %shard_map.59.refs_2_, f32[224,128]{1,0:T(8,128)S(1)} %collective-permute-done.7.refs_3_, ...), custom_call_target="tpu_custom_call" | custom-call | flops 10000000 | bytes 6569984 | tf_op jit(solution)/shard_map/pallas_call | solution.py:540
  21.0 0.2 collective-permute-start.9
  21.2 1.1 %collective-permute-done.9.refs_1_ = f32[4,16,128]{2,1,0:T(8,128)S(1)} collective-permute-done((f32[4,16,128]{2,1,0:T(8,128)S(1)}, f32[4,16,128]{2,1,0:T(8,128)S(1)}, u32[]{:S(2)}, u32[]{:S(2)}) %collective-permute-start.9) | collective-permute-done | bytes 32800 | tf_op jit(solution)/shard_map/ppermute | solution.py:564
  22.3 0.6 %shard_map.65 = f32[128,128]{1,0:T(8,128)} custom-call(f32[4,16,128]{2,1,0:T(8,128)S(1)} %get-tuple-element.27.refs_0_, f32[4,16,128]{2,1,0:T(8,128)S(1)} %collective-permute-done.9.refs_1_), custom_call_target="tpu_custom_call" | custom-call | bytes 131072 | tf_op jit(solution)/shard_map/pallas_call | solution.py:540
  (3 shorter events, 0.0 us)
Async XLA Ops:
  1.3 8.1 %collective-permute-start.1 = (f32[944,128]{1,0:T(8,128)S(1)}, f32[944,128]{1,0:T(8,128)S(1)}, u32[]{:S(2)}, u32[]{:S(2)}) collective-permute-start(f32[944,128]{1,0:T(8,128)S(1)} %get-tuple-element.22), channel_id=1, source_target_pairs={{0,2},{1,3},{2,0},{3,1},{4,6},{5,7},{6,4},{7,5},{8,10},{9,11},{10,... | collective-permute-start | bytes 1449992 | tf_op jit(solution)/shard_map/ppermute | solution.py:564
  1.9 7.5 %collective-permute-start = (f32[336,128]{1,0:T(8,128)S(1)}, f32[336,128]{1,0:T(8,128)S(1)}, u32[]{:S(2)}, u32[]{:S(2)}) collective-permute-start(f32[336,128]{1,0:T(8,128)S(1)} %get-tuple-element.21), channel_id=1, source_target_pairs={{0,1},{1,0},{2,3},{3,2},{4,5},{5,4},{6,7},{7,6},{8,9},{9,8},{10,11... | collective-permute-start | bytes 516104 | tf_op jit(solution)/shard_map/ppermute | solution.py:564
  4.4 10.2 %collective-permute-start.2 = (f32[176,128]{1,0:T(8,128)S(1)}, f32[176,128]{1,0:T(8,128)S(1)}, u32[]{:S(2)}, u32[]{:S(2)}) collective-permute-start(f32[176,128]{1,0:T(8,128)S(1)} %get-tuple-element.23), channel_id=1, source_target_pairs={{0,4},{1,5},{2,14},{3,15},{4,8},{5,9},{6,2},{7,3},{8,12},{9,13},{1... | collective-permute-start | bytes 270344 | tf_op jit(solution)/shard_map/ppermute | solution.py:564
  6.0 8.6 %collective-permute-start.3 = (f32[176,128]{1,0:T(8,128)S(1)}, f32[176,128]{1,0:T(8,128)S(1)}, u32[]{:S(2)}, u32[]{:S(2)}) collective-permute-start(f32[176,128]{1,0:T(8,128)S(1)} %get-tuple-element.24), channel_id=1, source_target_pairs={{0,14},{1,15},{2,4},{3,5},{4,2},{5,3},{6,8},{7,9},{8,6},{9,7},{10,... | collective-permute-start | bytes 270344 | tf_op jit(solution)/shard_map/ppermute | solution.py:564
  9.4 9.7 %collective-permute-start.6 = (f32[336,128]{1,0:T(8,128)S(1)}, f32[336,128]{1,0:T(8,128)S(1)}, u32[]{:S(2)}, u32[]{:S(2)}) collective-permute-start(f32[336,128]{1,0:T(8,128)S(1)} %collective-permute-done.refs_0_.refs_6_), channel_id=1, source_target_pairs={{0,2},{1,3},{2,0},{3,1},{4,6},{5,7},{6,4},{7,5},{8,10},{9,11},{10,... | collective-permute-start | bytes 516104 | tf_op jit(solution)/shard_map/ppermute | solution.py:564
  9.4 10.3 %collective-permute-start.8 = (f32[224,128]{1,0:T(8,128)S(1)}, f32[224,128]{1,0:T(8,128)S(1)}, u32[]{:S(2)}, u32[]{:S(2)}) collective-permute-start(f32[224,128]{1,0:T(8,128)S(1)} %pad_maximum_fusion.1), channel_id=1, source_target_pairs={{0,4},{1,5},{2,14},{3,15},{4,8},{5,9},{6,2},{7,3},{8,12},{9,13},{1... | collective-permute-start | bytes 344072 | tf_op jit(solution)/shard_map/ppermute | solution.py:564
  11.3 9.1 %collective-permute-start.7 = (f32[224,128]{1,0:T(8,128)S(1)}, f32[224,128]{1,0:T(8,128)S(1)}, u32[]{:S(2)}, u32[]{:S(2)}) collective-permute-start(f32[224,128]{1,0:T(8,128)S(1)} %pad_maximum_fusion), channel_id=1, source_target_pairs={{0,15},{1,14},{2,5},{3,4},{4,3},{5,2},{6,9},{7,8},{8,7},{9,6},{10,... | collective-permute-start | bytes 344072 | tf_op jit(solution)/shard_map/ppermute | solution.py:564
  14.6 3.8 %collective-permute-start.4 = (f32[176,128]{1,0:T(8,128)S(1)}, f32[176,128]{1,0:T(8,128)S(1)}, u32[]{:S(2)}, u32[]{:S(2)}) collective-permute-start(f32[176,128]{1,0:T(8,128)S(1)} %collective-permute-done.3.refs_2_), channel_id=1, source_target_pairs={{0,2},{1,3},{2,0},{3,1},{4,6},{5,7},{6,4},{7,5},{8,10},{9,11},{10,... | collective-permute-start | bytes 270344 | tf_op jit(solution)/shard_map/ppermute | solution.py:564
  14.6 3.8 %collective-permute-start.5 = (f32[176,128]{1,0:T(8,128)S(1)}, f32[176,128]{1,0:T(8,128)S(1)}, u32[]{:S(2)}, u32[]{:S(2)}) collective-permute-start(f32[176,128]{1,0:T(8,128)S(1)} %collective-permute-done.2.refs_1_), channel_id=1, source_target_pairs={{0,2},{1,3},{2,0},{3,1},{4,6},{5,7},{6,4},{7,5},{8,10},{9,11},{10,... | collective-permute-start | bytes 270344 | tf_op jit(solution)/shard_map/ppermute | solution.py:564
  21.0 1.3 %collective-permute-start.9 = (f32[4,16,128]{2,1,0:T(8,128)S(1)}, f32[4,16,128]{2,1,0:T(8,128)S(1)}, u32[]{:S(2)}, u32[]{:S(2)}) collective-permute-start(f32[4,16,128]{2,1,0:T(8,128)S(1)} %get-tuple-element.28), channel_id=1, source_target_pairs={{0,2},{1,3},{2,0},{3,1},{4,6},{5,7},{6,4},{7,5},{8,10},{9,11},{10,... | collective-permute-start | bytes 98312 | tf_op jit(solution)/shard_map/ppermute | solution.py:564
